TPU v7x, 32 devices: a whole 2x2x4 slice. The times are simulated.
32 devices in a mesh: dp: 2 (over x), seq: 4 (over y, core), mp: 4 (over z).
Axes of the slice: x: 2, y: 2, z: 4, core: 2. Of those that a mesh axis runs over, the one named last changes fastest.
Arguments:
- source: bfloat16 [4, 1024, 1024], P('dp', ('seq', 'mp')), may hold values from -6 to 6
- target: bfloat16 [4, 1024, 1024], P('dp', ('seq', 'mp')), may hold values from -6 to 6
- cotangent: bfloat16 [4, 1024, 1024], P('dp', ('seq', 'mp')), may hold values from -6 to 6
- source_len: int32 [4], P('dp'), may hold values from 512 to 1024, as said below
- target_len: int32 [4], P('dp'), may hold values from 512 to 1024, as said below
- source_seg: int32 [4, 1024], P('dp'), may hold values from 0 to 7, as said below
- target_seg: int32 [4, 1024], P('dp'), may hold values from 0 to 7, as said below
- enc_qkv: bfloat16 [3, 1024, 1024], P(None, ('dp', 'seq'), 'mp'), may hold values from -0.1875 to 0.1875
- enc_proj: bfloat16 [1024, 1024], P('mp', ('dp', 'seq')), may hold values from -0.75 to 0.75
- enc_up: bfloat16 [1024, 4096], P(('dp', 'seq'), 'mp'), may hold values from -0.1875 to 0.1875
- enc_down: bfloat16 [4096, 1024], P('mp', ('dp', 'seq')), may hold values from -0.125 to 0.125
- enc_gain: float32 [3, 1024], P(None, ('dp', 'seq', 'mp')), may hold values from 0.1 to 1.9
- enc_shift: float32 [3, 1024], P(None, ('dp', 'seq', 'mp')), may hold values from -1.8 to 1.8
- dec_qkv: bfloat16 [3, 1024, 1024], P(None, ('dp', 'seq'), 'mp'), may hold values from -0.1875 to 0.1875
- dec_proj: bfloat16 [1024, 1024], P('mp', ('dp', 'seq')), may hold values from -0.75 to 0.75
- cross_qkv: bfloat16 [3, 1024, 1024], P(None, ('dp', 'seq'), 'mp'), may hold values from -0.1875 to 0.1875
- cross_proj: bfloat16 [1024, 1024], P('mp', ('dp', 'seq')), may hold values from -0.75 to 0.75
- dec_up: bfloat16 [1024, 4096], P(('dp', 'seq'), 'mp'), may hold values from -0.1875 to 0.1875
- dec_down: bfloat16 [4096, 1024], P('mp', ('dp', 'seq')), may hold values from -0.125 to 0.125
- dec_gain: float32 [4, 1024], P(None, ('dp', 'seq', 'mp')), may hold values from 0.1 to 1.9
- dec_shift: float32 [4, 1024], P(None, ('dp', 'seq', 'mp')), may hold values from -1.8 to 1.8
Outputs:
- decoded: bfloat16 [4, 1024, 1024], P('dp', ('seq', 'mp'))
- source_grad: float32 [4, 1024, 1024], P('dp', ('seq', 'mp'))
- target_grad: float32 [4, 1024, 1024], P('dp', ('seq', 'mp'))
- grad_enc_qkv: float32 [3, 1024, 1024], P(None, ('dp', 'seq'), 'mp')
- grad_enc_proj: float32 [1024, 1024], P('mp', ('dp', 'seq'))
- grad_enc_up: float32 [1024, 4096], P(('dp', 'seq'), 'mp')
- grad_enc_down: float32 [4096, 1024], P('mp', ('dp', 'seq'))
- grad_enc_gain: float32 [3, 1024], P(None, ('dp', 'seq', 'mp'))
- grad_enc_shift: float32 [3, 1024], P(None, ('dp', 'seq', 'mp'))
- grad_dec_qkv: float32 [3, 1024, 1024], P(None, ('dp', 'seq'), 'mp')
- grad_dec_proj: float32 [1024, 1024], P('mp', ('dp', 'seq'))
- grad_cross_qkv: float32 [3, 1024, 1024], P(None, ('dp', 'seq'), 'mp')
- grad_cross_proj: float32 [1024, 1024], P('mp', ('dp', 'seq'))
- grad_dec_up: float32 [1024, 4096], P(('dp', 'seq'), 'mp')
- grad_dec_down: float32 [4096, 1024], P('mp', ('dp', 'seq'))
- grad_dec_gain: float32 [4, 1024], P(None, ('dp', 'seq', 'mp'))
- grad_dec_shift: float32 [4, 1024], P(None, ('dp', 'seq', 'mp'))
Inputs may be any that keep to these rules, and one draw needn't show every extreme that they name: `source_len`: rows of a slot from its length on are padding; some slot of every draw has 1024 live rows. `target_len`: rows of a slot from its length on are padding; some slot of every draw has 1024 live rows. `source_seg`: ids never fall along a slot. A slot holds one pair (id 0 throughout) or 8 pairs, each with live rows; padding rows carry the last id. A slot's source and target hold the same number of pairs, and some slot of every draw holds 8. `target_seg`: ids never fall along a slot. A slot holds one pair (id 0 throughout) or 8 pairs, each with live rows; padding rows carry the last id. A slot's source and target hold the same number of pairs, and some slot of every draw holds 8.
All inputs are finite; a program needn't handle non-finite values.
Results may differ from a plain program's by a relative error of at most 0.035.
Values may be sent and summed in bfloat16 or wider, within the bound.
A program may use at most 192 MiB of HBM per device.

v0:
```python
import math

import jax
import jax.numpy as jnp
from jax import lax
from jax.experimental import pallas as pl
from jax.experimental.pallas import tpu as pltpu
from jax.sharding import Mesh, PartitionSpec as P

HEAD_DIM = 64
EPSILON = 1e-05
MASKED = -1000000000.0
PAIRS = 8
AXES = ("hi", "k", "y", "c", "mp")
MESH_ID = pl.DeviceIdType.MESH
F32 = jnp.float32
BF16 = jnp.bfloat16


class Call:
    def __init__(self):
        self.known, self.arrays, self.specs = [], [], []
        self.shapes, self.places, self.scratch = [], [], []
        self.fetched, self.kept, self.rows_of = [], [], {}

    def take(self, array, space=pltpu.VMEM):
        if isinstance(array, tuple):
            return array
        for i, known in enumerate(self.known):
            if known is array and self.specs[i].memory_space == space:
                return ("in", i)
        self.known.append(array)
        if space == pltpu.HBM:
            array = pltpu.with_memory_space_constraint(array, pltpu.HBM)
        self.arrays.append(array)
        self.specs.append(pl.BlockSpec(memory_space=space))
        return ("in", len(self.arrays) - 1)

    def fetch(self, array):
        if isinstance(array, tuple):
            return array
        source = self.take(array, pltpu.HBM)
        for i, (known, room, sem) in enumerate(self.fetched):
            if known == source:
                return ("fetch", i)
        self.fetched.append((source, self.hold(array.shape, array.dtype), self.sems(1)))
        return ("fetch", len(self.fetched) - 1)

    def give(self, shape, dtype, space=pltpu.VMEM):
        if space == pltpu.HBM:
            self.shapes.append(pltpu.HBM(shape, dtype))
        else:
            self.shapes.append(jax.ShapeDtypeStruct(shape, dtype))
        self.places.append(pl.BlockSpec(memory_space=space))
        return ("out", len(self.shapes) - 1)

    def keep(self, shape, dtype, parts=1):
        target = self.give(shape, dtype, pltpu.HBM)
        self.kept.append((target, self.hold(shape, dtype), self.sems(parts)))
        return ("keep", len(self.kept) - 1)

    def hold(self, shape, dtype):
        self.scratch.append(pltpu.VMEM(shape, dtype))
        return ("tmp", len(self.scratch) - 1)

    def sems(self, count):
        self.scratch.append(pltpu.SemaphoreType.DMA((count,)))
        return ("tmp", len(self.scratch) - 1)

    def save(self, get, handle, row=None):
        target, room, sems = (get(part) for part in self.kept[handle[1]])
        if row is not None:
            target, room = target.at[row], room.at[row]
        count = sum(1 for known, unused in self.saves if known == handle)
        copy = pltpu.make_async_copy(room, target, sems.at[count])
        copy.start()
        self.saves.append((handle, copy))

    def run(self, body, name, collective=None, flops=0):
        ins, outs = len(self.arrays), len(self.shapes)

        def kernel(*refs):
            parts = {"in": refs[:ins], "out": refs[ins : ins + outs], "tmp": refs[ins + outs :]}
            here, self.saves, self.waited = set(), [], []

            def get(handle):
                kind, i = handle
                if kind == "keep":
                    return get(self.kept[i][1])
                if kind != "fetch":
                    return parts[kind][i]
                source, room, sem = (get(part) for part in self.fetched[i])
                if i not in here:
                    here.add(i)
                    pltpu.make_async_copy(source, room, sem.at[0]).wait()
                return room

            for source, room, sem in self.fetched:
                pltpu.make_async_copy(get(source), get(room), get(sem).at[0]).start()
            body(get)
            for i in range(len(self.fetched)):
                get(("fetch", i))
            for handle, copy in self.saves:
                copy.wait()

        held = [a for a, spec in zip(self.arrays, self.specs) if spec.memory_space == pltpu.VMEM]
        held += [a for a, spec in zip(self.shapes, self.places) if spec.memory_space == pltpu.VMEM]
        held += [x for x in self.scratch if x.dtype in (BF16, F32)]
        room = sum(math.prod(x.shape) * jnp.dtype(x.dtype).itemsize for x in held)
        return pl.pallas_call(
            kernel,
            out_shape=tuple(self.shapes),
            in_specs=self.specs,
            out_specs=tuple(self.places),
            scratch_shapes=self.scratch,
            compiler_params=pltpu.CompilerParams(
                collective_id=collective,
                has_side_effects=collective is not None,
                vmem_limit_bytes=room + (8 << 20),
            ),
            cost_estimate=pl.CostEstimate(flops=flops, bytes_accessed=0, transcendentals=0),
            name=name,
        )(*self.arrays)


MICROSECOND = 1_000_000_000


def nt(left, right):
    return lax.dot_general(left, right, (((1,), (1,)), ((), ())), preferred_element_type=F32)


def nn(left, right):
    return lax.dot_general(left, right, (((1,), (0,)), ((), ())), preferred_element_type=F32)


def tn(left, right):
    return lax.dot_general(left, right, (((0,), (0,)), ((), ())), preferred_element_type=F32)


def unit_of(stream):
    average = jnp.mean(stream, -1, keepdims=True)
    centred = stream - average
    scale = lax.rsqrt(jnp.mean(centred * centred, -1, keepdims=True) + EPSILON)
    return centred * scale, scale


def norm_back(stream, gain, upstream):
    unit, scale = unit_of(stream)
    inner = upstream * gain
    grad = scale * (
        inner - jnp.mean(inner, -1, keepdims=True) - unit * jnp.mean(inner * unit, -1, keepdims=True)
    )
    shares = jnp.concatenate(
        [jnp.sum(upstream * unit, 0, keepdims=True), jnp.sum(upstream, 0, keepdims=True)], 0
    )
    return grad, shares


def gelu_pair(act):
    bell = 0.5 + 0.5 * lax.erf(act * 0.7071067811865476)
    slope = bell + act * (jnp.exp(act * act * -0.5) * 0.3989422804014327)
    return act * bell, slope


def place():
    hi, k, y, c, z = (lax.axis_index(name) for name in AXES)
    return {
        "x": (1 - hi, k, y, c, z),
        "y": (hi, k, 1 - y, c, z),
        "d": (1 - hi, k, 1 - y, c, z),
        "core": (hi, k, y, 1 - c, z),
        "mesh": (hi, k, y, c, z),
        "own_row": y * 2 + hi,
        "x_row": y * 2 + 1 - hi,
        "y_row": (1 - y) * 2 + hi,
        "d_row": (1 - y) * 2 + 1 - hi,
    }


def greet(partners):
    barrier = pltpu.get_barrier_semaphore()
    for partner in partners:
        pl.semaphore_signal(barrier, inc=1, device_id=partner, device_id_type=MESH_ID)
    pl.semaphore_wait(barrier, len(partners))


def along(at):
    hi, k, y, c, z = at["mesh"]
    return [(hi, k, y, c, lax.rem(z + n, 4)) for n in range(1, 4)]


class Weight:
    def __init__(self, call, packed, first, count):
        self.call, self.source = call, call.take(packed, pltpu.HBM)
        self.room = call.hold((4, count, 1024), BF16)
        self.sem = call.sems(1)
        self.first, self.count = first, count

    def start(self, get):
        source, room, sem = get(self.source), get(self.room), get(self.sem)
        for q in range(4):
            for c in range(2):
                pltpu.make_async_copy(
                    source.at[c, :, q, pl.ds(self.first, self.count), :],
                    room.at[:, :, pl.ds((q * 2 + c) * 128, 128)],
                    sem.at[0],
                ).start()

    def wait(self, get):
        if self in self.call.waited:
            return
        self.call.waited.append(self)
        room = get(self.room)
        pltpu.make_async_copy(room, room, get(self.sem).at[0]).wait()

    def matrix(self, get, first, count):
        return get(self.room)[:, first : first + count, :].reshape(4 * count, 1024)


def stack(blocks):
    return blocks[0] if len(blocks) == 1 else jnp.concatenate(blocks, 0)


class Feed:
    def __init__(self, call, rows, up, down):
        self.call, self.rows, self.weights = call, call.fetch(rows), [up, down]
        self.hidden = call.keep((4, 128, 1024), BF16, 4)
        self.slope = call.keep((4, 128, 1024), F32, 4)

    def part(self, get, *rows):
        up, down = self.weights
        whole = stack([get(self.rows)[row] for row in rows])
        made, slope = gelu_pair(nt(whole, up.matrix(get, 0, 256)))
        made = made.astype(BF16)
        for i, row in enumerate(rows):
            get(self.hidden)[row] = made[i * 128 : (i + 1) * 128]
            get(self.slope)[row] = slope[i * 128 : (i + 1) * 128]
            self.call.save(get, self.hidden, row)
            self.call.save(get, self.slope, row)
        return nn(made, down.matrix(get, 0, 256))


class Job:
    def __init__(self, call, left, mid, right):
        self.call, self.left, self.mid, self.right = call, left, mid, right
        self.kept, self.shares = getattr(mid, "kept", None), getattr(mid, "shares", None)
        if left is not None:
            self.rows_in = None if isinstance(left, Feed) else call.fetch(left[0])
            self.out_first = call.hold((2, 128, 1024), BF16)
            self.out_edge = call.hold((2, 64, 1024), BF16)
            self.out_late = call.hold((2, 64, 1024), BF16)
            self.keep = call.hold((2, 64, 1024), F32)
            self.own = call.hold((128, 1024), F32)
            self.landed = call.hold((6, 64, 1024), BF16)
            self.sum_send, self.sum_recv = call.sems(6), call.sems(6)
        self.gathered = None
        if right is not None:
            self.gathered = call.keep((4, 128, 1024), BF16, 4)
            self.row_send, self.row_recv = call.sems(6), call.sems(6)

    def lefts(self):
        return self.left.weights if isinstance(self.left, Feed) else [self.left[1]]

    def part(self, get, *rows):
        if isinstance(self.left, Feed):
            return self.left.part(get, *rows)
        unused, weight, picks, column = self.left
        total = None
        for first, count in picks:
            width = 4 * count
            left = stack([get(self.rows_in)[row, :, column : column + width] for row in rows])
            term = nn(left, weight.matrix(get, first, count))
            total = term if total is None else total + term
            column += width
        return total

    def send(self, get, i, source, target, partner):
        copy = pltpu.make_async_remote_copy(
            src_ref=source,
            dst_ref=target,
            send_sem=get(self.sum_send).at[i],
            recv_sem=get(self.sum_recv).at[i],
            device_id=partner,
            device_id_type=MESH_ID,
        )
        copy.start()
        return copy

    def sum_start(self, get, at):
        first, edge, landed = get(self.out_first), get(self.out_edge), get(self.landed)
        keep = get(self.keep)
        self.copies = [None] * 6
        first[0] = self.part(get, at["d_row"]).astype(BF16)
        self.copies[0] = self.send(
            get, 0, first.at[0, pl.ds(0, 64)], landed.at[0], at["x"]
        )
        self.copies[1] = self.send(
            get, 1, first.at[0, pl.ds(64, 64)], landed.at[1], at["y"]
        )
        part = self.part(get, at["x_row"], at["y_row"])
        edge[0] = part[:64].astype(BF16)
        keep[0] = part[64:128]
        self.copies[2] = self.send(get, 2, edge.at[0], landed.at[2], at["x"])
        edge[1] = part[192:].astype(BF16)
        keep[1] = part[128:192]
        self.copies[3] = self.send(get, 3, edge.at[1], landed.at[3], at["y"])

    def sum_forward(self, get, at):
        late, landed, keep = get(self.out_late), get(self.landed), get(self.keep)
        self.copies[0].wait_recv()
        late[1] = (keep[1] + landed[0].astype(F32)).astype(BF16)
        self.copies[4] = self.send(get, 4, late.at[1], landed.at[4], at["y"])
        self.copies[1].wait_recv()
        late[0] = (keep[0] + landed[1].astype(F32)).astype(BF16)
        self.copies[5] = self.send(get, 5, late.at[0], landed.at[5], at["x"])

    def sum_own(self, get, at):
        get(self.own)[...] = self.part(get, at["own_row"])

    def sum_end(self, get):
        landed, own = get(self.landed), get(self.own)
        for i in (2, 3, 4, 5):
            self.copies[i].wait_recv()
        upper = own[:64] + landed[2].astype(F32) + landed[4].astype(F32)
        lower = own[64:] + landed[5].astype(F32) + landed[3].astype(F32)
        return jnp.concatenate([upper, lower], 0)

    def row_copy(self, get, i, row, half, partner):
        block = get(self.gathered).at[row, pl.ds(half * 64, 64)]
        copy = pltpu.make_async_remote_copy(
            src_ref=block,
            dst_ref=block,
            send_sem=get(self.row_send).at[i],
            recv_sem=get(self.row_recv).at[i],
            device_id=partner,
            device_id_type=MESH_ID,
        )
        copy.start()
        return copy

    def rows_start(self, get, at, normed):
        get(self.gathered)[at["own_row"]] = normed
        self.call.save(get, self.gathered, at["own_row"])
        self.moves = [
            self.row_copy(get, 0, at["own_row"], 0, at["y"]),
            self.row_copy(get, 1, at["own_row"], 1, at["x"]),
            self.row_copy(get, 2, at["own_row"], 1, at["y"]),
            self.row_copy(get, 3, at["own_row"], 0, at["x"]),
        ]

    def rows_forward(self, get, at):
        self.moves[0].wait_recv()
        self.moves.append(self.row_copy(get, 4, at["y_row"], 0, at["x"]))
        self.moves[1].wait_recv()
        self.moves.append(self.row_copy(get, 5, at["x_row"], 1, at["y"]))

    def product(self, get, at, row):
        weight, picks, store = self.right
        if weight is None:
            return
        weight.wait(get)
        rows = get(self.gathered)[row]
        column = 0
        for first, count in picks:
            store(get, at, row, column, nt(rows, weight.matrix(get, first, count)))
            column += 4 * count

    def sums(self, get, at):
        for weight in self.lefts():
            weight.wait(get)
        self.sum_start(get, at)

    def settle(self, get, at):
        normed = self.mid(get, self.sum_end(get) if self.left is not None else None)
        if self.right is not None:
            self.rows_start(get, at, normed)

    def collect(self, get, at, sides=True, far=True):
        for moves, row in (((3,), "x_row"), ((2,), "y_row"), ((4, 5), "d_row")):
            if far if row == "d_row" else sides:
                for i in moves:
                    self.moves[i].wait_recv()
                self.call.save(get, self.gathered, at[row])
                self.product(get, at, at[row])

    def drain(self):
        if self.left is not None:
            for copy in self.copies:
                copy.wait_send()
        if self.right is not None:
            for copy in self.moves:
                copy.wait_send()


def run_body(call, work, names, name, collective, flops):
    groups = {"all": meeting, "z": along, "ways": lambda at: all_partners(at)[1]}

    def body(get):
        at = place()
        partners = []
        for group in names:
            partners += groups[group](at) if group in groups else [at[group]]
        greet(partners)
        work(get, at)

    return call.run(body, name, collective, flops)


class Kept:
    def __init__(self, out, store):
        self.out, self.store = out, store


class Plain:
    def __init__(self, call, width):
        self.call, self.width = call, width
        self.out = call.keep((4, 128, width), BF16, 4)

    def store(self, get, at, row, column, value):
        get(self.out)[row, :, column : column + value.shape[1]] = value.astype(BF16)
        if column + value.shape[1] == self.width:
            self.call.save(get, self.out, row)


class Shared:
    def __init__(self, call, width, skip=0):
        self.call, self.out = call, call.keep((2, 4, 128, width), BF16, 2)
        self.send_sem, self.recv_sem = call.sems(4), call.sems(4)
        self.width, self.skip, self.copies, self.blocks = width, skip, [], 0

    def store(self, get, at, row, column, value):
        out = get(self.out)
        column = column - self.skip
        out[0, row, :, column : column + value.shape[1]] = value.astype(BF16)
        if column + value.shape[1] == self.width:
            i = len(self.copies)
            copy = pltpu.make_async_remote_copy(
                src_ref=out.at[0, row],
                dst_ref=out.at[1, row],
                send_sem=get(self.send_sem).at[i],
                recv_sem=get(self.recv_sem).at[i],
                device_id=at["core"],
                device_id_type=MESH_ID,
            )
            copy.start()
            self.copies.append(copy)

    def finish(self, get):
        self.call.save(get, self.out, 0)
        for copy in self.copies:
            copy.wait()
        self.call.save(get, self.out, 1)


def query_and_shared(call, width):
    query, shared = Plain(call, width), Shared(call, 2 * width, skip=width)

    def store(get, at, row, column, value):
        if column < width:
            query.store(get, at, row, column, value)
        else:
            shared.store(get, at, row, column, value)

    return store, shared.finish


def lanes_of(head, rows):
    lane = lax.broadcasted_iota(jnp.int32, (rows, 128), 1)
    return lane // HEAD_DIM == head


SOURCE, TARGET, PLACE, LIVE = 0, 1, 2, 3


def allowed_bias(rows, columns, query_kind, key_kind, causal):
    allowed = columns[:, key_kind : key_kind + 1] == rows[query_kind : query_kind + 1, :512]
    allowed = allowed & (columns[:, LIVE + key_kind : LIVE + key_kind + 1] > 0.5)
    if causal:
        allowed = allowed & (columns[:, PLACE : PLACE + 1] <= rows[PLACE : PLACE + 1, :512])
    return jnp.where(allowed, 0.0, MASKED)


def masked(mask, span, count):
    if count == 4:
        return mask[:, span]
    return jnp.concatenate([mask[: count * 128, span], mask[512 : 512 + count * 128, span]], 0)


class Attend:
    def __init__(self, call, queries, key_value, rows, columns, kinds):
        self.call, self.kinds = call, kinds
        self.queries, self.key_value = call.fetch(queries), call.fetch(key_value)
        self.rows, self.columns = call.take(rows), call.fetch(columns)
        self.mixed = call.keep((4, 128, 256), BF16)
        self.total = call.give((8, 512), F32)
        self.bias = call.hold((1024, 512), F32)

    def late(self, get, at):
        self.prepare(get)
        self.pairs(get, 0, 2)
        self.call.save(get, self.mixed)

    def visible(self, block):
        return 2 if self.kinds[2] and block == 0 else 4

    def prepare(self, get):
        mask = get(self.bias)
        mask[...] = allowed_bias(get(self.rows), get(self.columns), *self.kinds)

    def pairs(self, get, first, last):
        mask = get(self.bias)
        q_ref, kv_ref = get(self.queries), get(self.key_value)
        mixed_ref, total_ref = get(self.mixed), get(self.total)

        def pair_step(pair, carry):
            lanes = pl.ds(pl.multiple_of(pair * 128, 128), 128)
            value_lanes = pl.ds(pl.multiple_of(256 + pair * 128, 128), 128)
            for block in range(2):
                count = self.visible(block)
                keys = kv_ref[:, :count, :, lanes].reshape(count * 256, 128)
                values = kv_ref[:, :count, :, value_lanes].reshape(count * 256, 128)
                span = slice(block * 256, block * 256 + 256)
                queries = q_ref[2 * block : 2 * block + 2, :, lanes].reshape(256, 128)
                mixed = []
                for head in range(2):
                    picked = jnp.where(lanes_of(head, 256), queries * 0.125, 0.0).astype(BF16)
                    scores = nt(keys, picked) + masked(mask, span, count)
                    top = jnp.max(scores, 0, keepdims=True)
                    raised = jnp.exp(scores - top)
                    total = jnp.sum(raised, 0, keepdims=True)
                    probs = (raised * (1.0 / total)).astype(BF16)
                    mixed.append(tn(values, probs)[head * HEAD_DIM : (head + 1) * HEAD_DIM])
                    total_ref[pl.ds(pair * 2 + head, 1), span] = top + jnp.log(total)
                mixed = jnp.concatenate(mixed, 0).T.astype(BF16)
                mixed_ref[2 * block : 2 * block + 2, :, lanes] = mixed.reshape(2, 128, 128)
            return carry

        lax.fori_loop(first, last, pair_step, 0)


class AttendBack:
    def __init__(self, call, queries, key_value, grad_mixed, total, rows, columns, kinds):
        self.call, self.kinds = call, kinds
        self.queries, self.key_value = call.fetch(queries), call.fetch(key_value)
        self.grad_mixed, self.total = call.fetch(grad_mixed), call.take(total)
        self.rows, self.columns = call.take(rows), call.fetch(columns)
        self.out = call.keep((4, 128, 768), BF16)
        self.bias, self.sums = call.hold((1024, 512), F32), call.hold((1024, 512), F32)
        self.away, self.landed = call.hold((2, 512, 256), BF16), call.hold((2, 512, 256), BF16)
        self.send_sem, self.recv_sem = call.sems(2), call.sems(2)

    def partners(self, at):
        return [at["core"]]

    def late(self, get, at):
        self.prepare(get)
        for pair in range(2):
            self.pair(get, at, pair)
        self.end(get)

    def prepare(self, get):
        mask = get(self.bias)
        mask[...] = allowed_bias(get(self.rows), get(self.columns), *self.kinds)
        self.copies = []

    def pair(self, get, at, pair):
        out, mask, sums = get(self.out), get(self.bias), get(self.sums)
        away, here = get(self.away), get(self.landed)
        q_ref, kv_ref = get(self.queries), get(self.key_value)
        grad_ref, total_ref = get(self.grad_mixed), get(self.total)
        lanes = slice(pair * 128, pair * 128 + 128)
        key_sum = slice(pair * 256, pair * 256 + 128)
        value_sum = slice(pair * 256 + 128, pair * 256 + 256)
        for block in (1, 0):
            count = 2 if self.kinds[2] and block == 0 else 4
            keys_pair = kv_ref[:, :count, :, lanes].reshape(count * 256, 128)
            values_pair = kv_ref[:, :count, :, 256 + pair * 128 : 384 + pair * 128]
            values_pair = values_pair.reshape(count * 256, 128)
            span = slice(block * 256, block * 256 + 256)
            two = slice(2 * block, 2 * block + 2)
            q_block = q_ref[two, :, lanes].reshape(256, 128)
            g_block = grad_ref[two, :, lanes].reshape(256, 128)
            grad_query = []
            for head in range(2):
                inside = lanes_of(head, 256)
                picked = jnp.where(inside, q_block * 1.0, 0.0).astype(BF16)
                grads = jnp.where(inside, g_block * 1.0, 0.0).astype(BF16)
                scores = nt(keys_pair, picked) * 0.125 + masked(mask, span, count)
                probs = jnp.exp(scores - total_ref[pair * 2 + head : pair * 2 + head + 1, span])
                weighted = probs * nt(values_pair, grads)
                inner = jnp.sum(weighted, 0, keepdims=True)
                grad_raw = ((weighted - probs * inner) * 0.125).astype(BF16)
                value_term = nn(probs.astype(BF16), grads)
                key_term = nn(grad_raw, picked)
                if block == 1 and head == 0:
                    sums[:, key_sum] = key_term
                    sums[:, value_sum] = value_term
                else:
                    for half in range(2 if count < 4 else 1):
                        size = count * 128 if count < 4 else 1024
                        rows = slice(half * 512, half * 512 + size)
                        terms = slice(half * size, half * size + size)
                        sums[rows, key_sum] += key_term[terms]
                        sums[rows, value_sum] += value_term[terms]
                grad_query.append(tn(keys_pair, grad_raw)[head * HEAD_DIM : (head + 1) * HEAD_DIM])
            grad_query = jnp.concatenate(grad_query, 0).T.astype(BF16)
            out[two, :, lanes] = grad_query.reshape(2, 128, 128)
        away[pair] = sums[512:, pair * 256 : pair * 256 + 256].astype(BF16)
        copy = pltpu.make_async_remote_copy(
            src_ref=away.at[pair],
            dst_ref=here.at[pair],
            send_sem=get(self.send_sem).at[pair],
            recv_sem=get(self.recv_sem).at[pair],
            device_id=at["core"],
            device_id_type=MESH_ID,
        )
        copy.start()
        self.copies.append(copy)

    def end(self, get):
        out, sums, here = get(self.out), get(self.sums), get(self.landed)
        for pair in range(2):
            self.copies[pair].wait()
            both = sums[:512, pair * 256 : pair * 256 + 256] + here[pair].astype(F32)
            both = both.astype(BF16).reshape(4, 128, 256)
            out[:, :, 256 + pair * 128 : 384 + pair * 128] = both[:, :, :128]
            out[:, :, 512 + pair * 128 : 640 + pair * 128] = both[:, :, 128:]
        self.call.save(get, self.out)


class Shares:
    def __init__(self, call, pairs, count, out=None, base=0):
        self.call, self.count, self.base = call, count, base
        self.handles = [
            (call.fetch(left), column, call.fetch(right))
            for left, column, right in pairs
        ]
        shape = (4, 4, len(pairs) * count, 128)
        sends = len(pairs) * max(1, count // 64)
        self.made, self.landed = call.hold((2,) + shape, BF16), call.hold(shape, BF16)
        self.send_sem, self.recv_sem = call.sems(sends), call.sems(sends)
        self.rows = shape[2]
        self.out = call.give(shape, BF16, pltpu.HBM) if out is None else out
        self.saved = out is not False
        self.room, self.save_sem = call.hold(shape, BF16), call.sems(1)

    def partners(self, at):
        return [at["core"]]

    def send(self, get, at, part):
        i = len(self.copies)
        copy = pltpu.make_async_remote_copy(
            src_ref=get(self.made).at[(1 - lax.axis_index("c"),) + part],
            dst_ref=get(self.landed).at[part],
            send_sem=get(self.send_sem).at[i],
            recv_sem=get(self.recv_sem).at[i],
            device_id=at["core"],
            device_id_type=MESH_ID,
        )
        copy.start()
        self.copies.append((part, copy))

    def middle(self, get, at):
        self.copies, every, count = [], slice(None), self.count
        made = get(self.made)
        for m, (left, column, right) in enumerate(self.handles):
            left, right = get(left), get(right)
            span = slice(m * count, (m + 1) * count)
            for first in range(0, 4 * count, 256):
                start = column + first
                product = tn(
                    left[:, :, start : start + 256].reshape(512, 256), right[...].reshape(512, 1024)
                )
                for inner in range(0, 256, count):
                    z = (first + inner) // count
                    for d in range(8):
                        made[d % 2, z, d // 2, span, :] = product[
                            inner : inner + count, d * 128 : d * 128 + 128
                        ].astype(BF16)
                if count == 256:
                    self.send(get, at, (first // 256, every, pl.ds(m * count, count)))
            if count < 256:
                self.send(get, at, (every, every, pl.ds(m * count, count)))

    def finish(self, get, at):
        core = lax.axis_index("c")
        for part, copy in self.copies:
            copy.wait()
            own = get(self.made)[(core,) + part].astype(F32)
            get(self.room)[part] = (own + get(self.landed)[part].astype(F32)).astype(BF16)
        if not self.saved:
            return
        target = get(self.out).at[:, :, pl.ds(self.base, self.rows)]
        copy = pltpu.make_async_copy(get(self.room), target, get(self.save_sem).at[0])
        copy.start()
        self.call.saves.append((None, copy))


def push(source, target, send_sem, recv_sem, partner):
    return pltpu.make_async_remote_copy(
        src_ref=source,
        dst_ref=target,
        send_sem=send_sem,
        recv_sem=recv_sem,
        device_id=partner,
        device_id_type=MESH_ID,
    )


class Spread:
    def __init__(self, call, pack):
        rows = pack.shape if not isinstance(pack, tuple) else (4, call.rows_of[pack], 128)
        self.pack = call.take(pack, pltpu.HBM)
        self.out = call.give((2, 4) + tuple(rows), BF16, pltpu.HBM)
        self.send_sem, self.recv_sem = call.sems(5), call.sems(5)
        self.core_send, self.core_recv, self.own_sem = call.sems(6), call.sems(6), call.sems(1)

    def block(self, get, at, origin):
        return get(self.out).at[at["mesh"][3], origin]

    def move(self, get, at, way):
        hi, k, y, c, z = at["mesh"]
        step = {0: 1, 1: -1, 2: 2, 3: -2, 4: jnp.where(z == 2, 1, -1)}[way]
        origin = jnp.where(z == 2, 0, 3) if way == 4 else z
        target = self.block(get, at, origin)
        return push(
            target if way == 4 else get(self.pack),
            target,
            get(self.send_sem).at[way],
            get(self.recv_sem).at[way],
            (hi, k, y, c, lax.rem(z + step + 4, 4)),
        )

    def sends(self, at, way):
        z = at["mesh"][4]
        middle = (z == 1) | (z == 2)
        return {0: z < 3, 1: z > 0, 2: z < 2, 3: z > 1, 4: middle}[way]

    def comes(self, at, way):
        z = at["mesh"][4]
        return {0: z > 0, 1: z < 3, 2: z > 1, 3: z < 2, 4: (z == 0) | (z == 3)}[way]

    def to_core(self, get, at, way):
        z = at["mesh"][4]
        origin = {0: z - 1, 1: z + 1, 2: z - 2, 3: z + 2, 4: 3 - z, 5: z}[way]
        target = self.block(get, at, origin)
        return push(
            get(self.pack) if way == 5 else target,
            target,
            get(self.core_send).at[way],
            get(self.core_recv).at[way],
            at["core"],
        )

    def own(self, get, at):
        return pltpu.make_async_copy(
            get(self.pack), self.block(get, at, at["mesh"][4]), get(self.own_sem).at[0]
        )

    def launch(self, get, at):
        for way in (2, 3, 0, 1):

            @pl.when(self.sends(at, way))
            def _():
                self.move(get, at, way).start()

        self.to_core(get, at, 5).start()
        self.own(get, at).start()

    def relay(self, get, at):
        for plane, way in ((2, 2), (1, 3)):

            @pl.when(at["mesh"][4] == plane)
            def _():
                self.move(get, at, way).wait_recv()
                self.move(get, at, 4).start()
                self.to_core(get, at, way).start()

    def pass_on(self, get, at):
        z = at["mesh"][4]
        for way in (0, 1, 2, 3, 4):
            taken = {2: z == 2, 3: z == 1}.get(way, z < 0)

            @pl.when(self.comes(at, way) & jnp.logical_not(taken))
            def _():
                self.move(get, at, way).wait_recv()
                self.to_core(get, at, way).start()

    def finish(self, get, at):
        self.own(get, at).wait()
        self.to_core(get, at, 5).wait()
        for way in range(5):

            @pl.when(self.comes(at, way))
            def _():
                self.to_core(get, at, way).wait()

            @pl.when(self.sends(at, way))
            def _():
                self.move(get, at, way).wait_send()


class Gather:
    def __init__(self, call, shares, rows, first=0):
        self.call, self.shares, self.rows, self.first = call, call.take(shares, pltpu.HBM), rows, first
        self.landed, self.own = call.hold((3, 4, rows, 128), BF16), call.hold((4, rows, 128), BF16)
        self.far, self.room = call.hold((4, rows, 128), BF16), call.hold((4, rows, 128), BF16)
        self.out = call.keep((4, rows, 128), BF16)
        self.send_sem, self.recv_sem, self.own_sem = call.sems(4), call.sems(4), call.sems(2)

    def share(self, get, plane):
        return get(self.shares).at[plane, :, pl.ds(self.first, self.rows)]

    def move(self, get, at, way, summed=False):
        hi, k, y, c, z = at["mesh"]
        step = {0: 1, 1: 3, 2: 2, 3: jnp.where(z == 0, 1, 3)}[way]
        partner = lax.rem(z + step, 4)
        source = self.share(get, 3 - z if way == 3 else partner)
        return push(
            get(self.room) if summed else source,
            get(self.room) if way == 3 else get(self.landed).at[way],
            get(self.send_sem).at[way],
            get(self.recv_sem).at[way],
            (hi, k, y, c, partner),
        )

    def local(self, get, at, far):
        z = at["mesh"][4]
        return pltpu.make_async_copy(
            self.share(get, lax.rem(z + 2, 4) if far else z),
            get(self.far if far else self.own),
            get(self.own_sem).at[1 if far else 0],
        )

    def launch(self, get, at):
        z = at["mesh"][4]
        outer = (z == 0) | (z == 3)
        for way, when in ((3, outer), (2, outer), (0, z < 3), (1, z > 0)):

            @pl.when(when)
            def _():
                self.move(get, at, way).start()

        for far in (False, True):
            self.local(get, at, far).start()

    def relay(self, get, at):
        z = at["mesh"][4]

        @pl.when((z == 1) | (z == 2))
        def _():
            self.move(get, at, 3).wait_recv()
            self.local(get, at, True).wait()
            room = get(self.room)
            room[...] = (room[...].astype(F32) + get(self.far)[...].astype(F32)).astype(BF16)
            self.move(get, at, 2, True).start()

        @pl.when((z == 0) | (z == 3))
        def _():
            self.local(get, at, True).wait()

    def finish(self, get, at):
        z = at["mesh"][4]
        landed, own, out = get(self.landed), get(self.own), get(self.out)
        self.local(get, at, False).wait()
        self.move(get, at, 2).wait()
        for which, ways in ((z == 0, (1,)), (z == 3, (0,)), ((z == 1) | (z == 2), (0, 1))):

            @pl.when(which)
            def _():
                for way in ways:
                    self.move(get, at, way).wait_recv()
                for q in range(4):
                    total = own[q].astype(F32) + landed[2, q].astype(F32)
                    for way in ways:
                        total = total + landed[way, q].astype(F32)
                    out[q] = total.astype(BF16)

        self.call.save(get, self.out)
        for way, when in ((3, (z == 0) | (z == 3)), (0, z < 3), (1, z > 0)):

            @pl.when(when)
            def _():
                self.move(get, at, way).wait_send()


class Swap:
    def __init__(self, call, pack):
        self.pack = call.take(pack, pltpu.HBM)
        rows = call.rows_of[pack] if isinstance(pack, tuple) else pack.shape[1]
        self.out = call.give((4, rows, 128), BF16, pltpu.HBM)
        call.rows_of[self.out] = rows
        self.send_sem, self.recv_sem, self.own_sem = call.sems(3), call.sems(3), call.sems(1)

    def start(self, get, at):
        hi, k, y, c, z = at["mesh"]
        own = hi * 2 + y
        pack, out = get(self.pack), get(self.out)
        self.copies = [pltpu.make_async_copy(pack.at[own], out.at[own], get(self.own_sem).at[0])]
        for i, (name, q) in enumerate(
            (("d", (1 - hi) * 2 + 1 - y), ("x", (1 - hi) * 2 + y), ("y", hi * 2 + 1 - y))
        ):
            send, recv = get(self.send_sem).at[i], get(self.recv_sem).at[i]
            self.copies.append(push(pack.at[q], out.at[own], send, recv, at[name]))
        for copy in self.copies:
            copy.start()

    def finish(self, get, at):
        for copy in self.copies:
            copy.wait()


class Slots:
    def __init__(self, call, arrays, inward):
        self.inward = inward
        self.call, self.arrays = call, [call.fetch(array) for array in arrays]
        shape = (128, 1024) if inward else (2, 64, 1024)
        self.outs = [call.keep(shape, BF16) for array in arrays]
        self.send_sem, self.recv_sem = call.sems(2 * len(arrays)), call.sems(2 * len(arrays))

    def ends(self, get, at, j, step):
        z = at["mesh"][4]
        low = lax.div(z, 2)
        other = low if step == 0 else 1 - low
        array, out = get(self.arrays[j]), get(self.outs[j])
        if self.inward:
            return array.at[other], out.at[pl.ds(pl.multiple_of(low * 64, 64), 64)]
        return array.at[pl.ds(pl.multiple_of(other * 64, 64), 64)], out.at[low]

    def stays(self, at):
        hi, z = at["mesh"][0], at["mesh"][4]
        return lax.rem(z, 2) == hi

    def copy(self, get, at, j, step):
        hi, k, y, c, z = at["mesh"]
        low = lax.div(z, 2)
        partner = (lax.rem(z, 2), k, y, c, 2 * (low if step == 0 else 1 - low) + hi)
        source, target = self.ends(get, at, j, step)
        return pltpu.make_async_remote_copy(
            src_ref=source,
            dst_ref=target,
            send_sem=get(self.send_sem).at[2 * j + step],
            recv_sem=get(self.recv_sem).at[2 * j + step],
            device_id=partner,
            device_id_type=MESH_ID,
        )

    def start(self, get, at):
        stays = self.stays(at)
        for j in range(len(self.arrays)):
            self.copy(get, at, j, 1).start()

        @pl.when(jnp.logical_not(stays))
        def _():
            for j in range(len(self.arrays)):
                self.copy(get, at, j, 0).start()

        @pl.when(stays)
        def _():
            for j in range(len(self.arrays)):
                source, target = self.ends(get, at, j, 0)
                target[...] = source[...]

    def finish(self, get, at):
        for j in range(len(self.arrays)):
            self.copy(get, at, j, 1).wait()

        @pl.when(jnp.logical_not(self.stays(at)))
        def _():
            for j in range(len(self.arrays)):
                self.copy(get, at, j, 0).wait()

        for out in self.outs:
            self.call.save(get, out)


def all_partners(at):
    hi, k, y, c, z = at["mesh"]
    plane = [
        ((hi + i) % 2, k, (y + j) % 2, (c + n) % 2, z)
        for i in range(2)
        for j in range(2)
        for n in range(2)
        if i + j + n > 0
    ]
    ways = [((hi + i) % 2, k, y, c, (z + n) % 4) for i in range(2) for n in range(1, 4)]
    return plane, ways


def meeting(at):
    plane, ways = all_partners(at)
    return plane + ways


class Vectors:
    def __init__(self, call, vectors, inward):
        self.inward = inward
        self.source = call.take(vectors)
        self.out = call.give((16, 1024) if inward else (16, 128), F32)
        self.landed, self.whole = call.hold((7, 16, 128), F32), call.hold((16, 128), F32)
        self.split, self.along = call.hold((8, 16, 128), F32), call.hold((3, 16, 128), F32)
        self.send_sem, self.recv_sem = call.sems(10), call.sems(10)

    def move(self, get, i, source, target, partner):
        return push(source, target, get(self.send_sem).at[i], get(self.recv_sem).at[i], partner)

    def planes(self, get, at, source):
        return [
            self.move(get, n, source, get(self.along).at[n], partner)
            for n, partner in enumerate(along(at))
        ]

    def block(self, at):
        hi, k, y, c, z = at["mesh"]
        return (hi * 2 + y) * 2 + c

    def start(self, get, at):
        plane = all_partners(at)[0]
        if self.inward:
            self.copies = self.planes(get, at, get(self.source))
        else:
            split = get(self.split)
            for d in range(8):
                split[d] = get(self.source)[:, d * 128 : d * 128 + 128]
            self.copies = [
                self.move(
                    get,
                    3 + i,
                    split.at[(partner[0] * 2 + partner[2]) * 2 + partner[3]],
                    get(self.landed).at[i],
                    partner,
                )
                for i, partner in enumerate(plane)
            ]
        for copy in self.copies:
            copy.start()

    def second(self, get, at):
        plane = all_partners(at)[0]
        for copy in self.copies:
            copy.wait()
        whole, out = get(self.whole), get(self.out)
        if self.inward:
            whole[...] = get(self.source)[...] + jnp.sum(get(self.along)[...], 0)
            block = pl.ds(pl.multiple_of(self.block(at) * 128, 128), 128)
            out[:, block] = whole[...]
            self.copies = [
                self.move(get, 3 + i, whole, out.at[:, block], partner)
                for i, partner in enumerate(plane)
            ]
        else:
            whole[...] = get(self.split)[self.block(at)] + jnp.sum(get(self.landed)[...], 0)
            self.copies = self.planes(get, at, whole)
        for copy in self.copies:
            copy.start()

    def finish(self, get, at):
        for copy in self.copies:
            copy.wait()
        if not self.inward:
            get(self.out)[...] = get(self.whole)[...] + jnp.sum(get(self.along)[...], 0)


class Pack:
    def __init__(self, call, matrices):
        self.parts = [(call.fetch(array), index, across) for array, index, across in matrices]
        counts = [
            (array.shape[-1] if across else array.shape[-2]) // 4
            for array, index, across in matrices
        ]
        self.counts = counts
        self.out = call.hold((4, sum(counts), 128), BF16)
        call.rows_of[self.out] = sum(counts)

    def make(self, get):
        out, base = get(self.out), 0
        for (part, index, across), count in zip(self.parts, self.counts, strict=True):
            part = get(part)
            whole = part[...] if index is None else part[index]
            if across:
                whole = whole.astype(F32).T.astype(BF16)
            out[:, base : base + count, :] = whole.reshape(4, count, 128)
            base += count


def by_owner(rows, back=False):
    copies = lax.axis_size("k")
    if copies == 1:
        return rows
    shape, width = rows.shape, 128 // copies
    if back:
        rows = rows.reshape(-1, 2, 2, 2, copies, width).transpose(0, 1, 4, 2, 3, 5)
    else:
        rows = rows.reshape(-1, 2, copies, 2, 2, width).transpose(0, 1, 3, 4, 2, 5)
    return rows.reshape(shape)


def unpacked(packs, rows, wide):
    call = Call()
    rows_in = [call.fetch(array) for array in rows]
    ins = [call.fetch(array) for array in packs]
    plans = []
    for handle, array, kinds in zip(ins, packs, wide, strict=True):
        base = 0
        for kind in kinds:
            count = 256 if kind in ("up", "down") else 64
            if kind == "q":
                out = call.give((3, 128, 256), F32)
                plans += [(handle, base + i * 64, 64, out, i, True) for i in range(3)]
                base += 192
                continue
            shape = (128, 4 * count) if kind == "up" else (4 * count, 128)
            plans.append((handle, base, count, call.give(shape, F32), None, kind == "up"))
            base += count
    outs = [call.give(array.shape, F32) for array in rows]

    def body(get):
        for handle, base, count, out, index, across in plans:
            whole = get(handle)[:, base : base + count, :].astype(F32).reshape(4 * count, 128)
            whole = whole.T if across else whole
            if index is None:
                get(out)[...] = whole
            else:
                get(out)[index] = whole
        for source, out in zip(rows_in, outs, strict=True):
            get(out)[...] = get(source)[...].astype(F32)

    return call.run(body, "unpacked", None, 4 * MICROSECOND)


def local(
    source,
    target,
    cotangent,
    source_len,
    target_len,
    source_seg,
    target_seg,
    enc_qkv,
    enc_proj,
    enc_up,
    enc_down,
    enc_gain,
    enc_shift,
    dec_qkv,
    dec_proj,
    cross_qkv,
    cross_proj,
    dec_up,
    dec_down,
    dec_gain,
    dec_shift,
):
    copies, z = lax.axis_size("k"), lax.axis_index("mp")
    norms = (enc_gain, enc_shift, dec_gain, dec_shift)
    if copies > 1:
        norms = [lax.all_gather(vector, "k", axis=1, tiled=True) for vector in norms]

    def widen(array, axis):
        return array if copies == 1 else lax.all_gather(array, "k", axis=axis, tiled=True)

    enc_qkv, dec_qkv, cross_qkv = (widen(array, 1) for array in (enc_qkv, dec_qkv, cross_qkv))
    enc_proj, dec_proj, cross_proj = (widen(array, 1) for array in (enc_proj, dec_proj, cross_proj))
    enc_up, dec_up = widen(enc_up, 0), widen(dec_up, 0)
    enc_down, dec_down = widen(enc_down, 1), widen(dec_down, 1)

    ENC_G, ENC_B, DEC_G, DEC_B = 0, 3, 6, 10
    SELF, SELF_O = 192, 64
    Q, QKV, KV, O, FIRST_O = (0, 64), (0, 192), (64, 128), (192, 64), (0, 64)
    UP, DOWN = (0, 256), (256, 256)

    def pick(call, packed, span, base=0):
        return Weight(call, packed, base + span[0], span[1])

    def forward_mid(call, residual, gain, shift, normed=None):
        vec, res = call.take(vectors), call.fetch(residual)
        kept = call.keep((128, 1024), F32)

        def mid(get, total):
            stream = get(res)[...].astype(F32) + total
            get(kept)[...] = stream
            call.save(get, kept)
            unit, scale = unit_of(stream)
            made = (unit * get(vec)[gain : gain + 1] + get(vec)[shift : shift + 1]).astype(BF16)
            if normed is not None:
                get(normed)[...] = made
                call.save(get, normed)
            return made

        mid.kept = kept
        return mid

    def backward_mid(call, stream, gain, residual=None, dtype=F32):
        vec, kept = call.take(vectors), call.fetch(stream)
        res = None if residual is None else call.fetch(residual)
        grad_out, share_out = call.keep((128, 1024), dtype), call.give((2, 1024), F32)

        def mid(get, total):
            grad, shares = norm_back(get(kept)[...].astype(F32), get(vec)[gain : gain + 1], total)
            if res is not None:
                grad = grad + get(res)[...]
            get(grad_out)[...] = grad.astype(dtype)
            call.save(get, grad_out)
            get(share_out)[...] = shares
            return grad.astype(BF16)

        mid.kept, mid.shares = grad_out, share_out
        return mid

    def deactivated(call, slope):
        out = call.keep((4, 128, 1024), BF16, 4)

        def store(get, at, row, column, value):
            get(out)[row] = (value * get(slope)[row]).astype(BF16)
            call.save(get, out, row)

        return Kept(out, store)

    call = Call()
    slots = Slots(call, [by_owner(source), by_owner(target)], True)
    stream_h, target_h = slots.outs
    norm_parts, norm_own = [call.take(vector) for vector in norms], call.hold((16, 128), F32)
    first_vectors = Vectors(call, norm_own, True)
    fact_ids = [call.take(source_seg), call.take(target_seg)]
    fact_lengths = [call.take(source_len, pltpu.SMEM), call.take(target_len, pltpu.SMEM)]
    fact_own, fact_room = call.hold((2, 8, 128), F32), call.hold((2, 8, 128), F32)
    fact_rows, fact_columns = call.give((8, 1024), F32), call.keep((1024, 128), F32)
    fact_send, fact_recv = call.sems(1), call.sems(1)

    def three(array):
        return [(array, i, True) for i in range(3)]

    pack_1 = Pack(call, three(enc_qkv) + three(dec_qkv))
    pack_o = Pack(call, [(enc_proj, None, False), (dec_proj, None, False)])
    pack_2 = Pack(call, [(enc_up, None, True), (enc_down, None, False)])
    pack_3 = Pack(call, three(cross_qkv) + [(cross_proj, None, False)])
    pack_4 = Pack(call, [(dec_up, None, True), (dec_down, None, False)])
    swap_1, swap_o, swap_2, swap_3, swap_4 = (
        Swap(call, pack.out) for pack in (pack_1, pack_o, pack_2, pack_3, pack_4)
    )
    spread_1, spread_o, spread_2, spread_3, spread_4 = (
        Spread(call, swap.out) for swap in (swap_1, swap_o, swap_2, swap_3, swap_4)
    )

    def count_facts(get):
        own = get(fact_own)
        own[...] = jnp.zeros_like(own)
        lane = lax.broadcasted_iota(jnp.int32, (2, 128), 1)
        for kind in range(2):
            ids, lengths = get(fact_ids[kind])[...], get(fact_lengths[kind])
            table = jnp.zeros((2, 128), F32)
            for p in range(1, PAIRS):
                before = jnp.sum((ids < p).astype(F32), 1, keepdims=True)
                table = table + jnp.where(lane == p, before, 0.0)
            for slot in range(2):
                length = lengths[slot].astype(F32)
                own[slot, kind : kind + 1] = jnp.where(
                    lane[:1] == 0, length, table[slot : slot + 1]
                )

    def place_norms(get, at):
        z, total, row = at["mesh"][4], get(norm_own), 0
        total[...] = jnp.zeros_like(total)
        lane = lax.broadcasted_iota(jnp.int32, (1, 128), 1)
        width = 32 // copies
        for part in norm_parts:
            given = get(part)[...]
            pieces = [given[:, i * width : (i + 1) * width] for i in range(copies) for _ in range(4)]
            wide = jnp.concatenate(pieces, 1)
            total[row : row + given.shape[0]] = jnp.where((lane // width) % 4 == z, wide, 0.0)
            row += given.shape[0]

    def place_facts(get, at):
        hi, k, y, c, z = at["mesh"]
        slot = lax.div(z, 2)
        table = jnp.where(lax.rem(z, 2) == hi, get(fact_own)[slot], get(fact_room)[slot])

        def kinds(index):
            core = jnp.where(index < 512, c, 1 - c)
            part = index % 512
            place = (part // 256) * 512 + core * 256 + ((part // 64) % 2) * 128
            place = (place + ((part // 128) % 2) * 64 + part % 64).astype(F32)
            found = []
            for row in range(2):
                ids = jnp.zeros_like(place)
                for p in range(1, PAIRS):
                    ids = ids + jnp.where(place >= table[row : row + 1, p : p + 1], 1.0, 0.0)
                found.append(ids)
            live = [jnp.where(place < table[row : row + 1, 0:1], 1.0, 0.0) for row in range(2)]
            return found + [place] + live

        across = kinds(lax.broadcasted_iota(jnp.int32, (1, 1024), 1))
        down = kinds(lax.broadcasted_iota(jnp.int32, (1024, 128), 0))
        rows, columns = get(fact_rows), get(fact_columns)
        rows[...] = jnp.zeros_like(rows)
        lane = lax.broadcasted_iota(jnp.int32, (1024, 128), 1)
        wide = jnp.zeros((1024, 128), F32)
        for i in range(5):
            rows[i : i + 1] = across[i]
            wide = jnp.where(lane == i, down[i], wide)
        columns[...] = wide
        call.save(get, fact_columns)

    def first_mid(stream, gain, shift):
        def mid(get, total):
            unit, scale = unit_of(get(stream)[...].astype(F32))
            vec = get(first_vectors.out)
            return (unit * vec[gain : gain + 1] + vec[shift : shift + 1]).astype(BF16)

        return mid

    job_a = Job(call, None, first_mid(stream_h, ENC_G, ENC_B), (None, None, None))
    job_c = Job(call, None, first_mid(target_h, DEC_G, DEC_B), (None, None, None))
    vectors = first_vectors.out

    plans = []
    for rows, base in ((job_a.gathered, 0), (job_c.gathered, SELF)):
        query, shared = Plain(call, 256), Shared(call, 512, 256)
        plans.append((call.fetch(rows), pick(call, spread_1.out, QKV, base), query, shared))
    enc_step = Attend(
        call, plans[0][2].out, plans[0][3].out, fact_rows, fact_columns, (SOURCE, SOURCE, False)
    )
    self_step = Attend(
        call, plans[1][2].out, plans[1][3].out, fact_rows, fact_columns, (TARGET, TARGET, True)
    )
    enc_o, self_o = pick(call, spread_o.out, FIRST_O), pick(call, spread_o.out, FIRST_O, SELF_O)
    mid = forward_mid(call, stream_h, ENC_G + 1, ENC_B + 1)
    job_b = Job(call, (enc_step.mixed, enc_o, [(0, 64)], 0), mid, (None, None, None))
    mid = forward_mid(call, target_h, DEC_G + 1, DEC_B + 1)
    cross_a, cross_b = pick(call, spread_3.out, Q), pick(call, spread_3.out, KV)
    cross_o = pick(call, spread_3.out, O)
    query, shared = Plain(call, 256), Shared(call, 512)
    job_d = Job(call, (self_step.mixed, self_o, [(0, 64)], 0), mid, (cross_a, [(0, 64)], query.store))
    enc_u, enc_d = pick(call, spread_2.out, UP), pick(call, spread_2.out, DOWN)
    feed = Feed(call, job_b.gathered, enc_u, enc_d)
    mid = forward_mid(call, job_b.kept, ENC_G + 2, ENC_B + 2)
    job_m = Job(call, feed, mid, (cross_b, [(0, 64), (64, 64)], shared.store))
    cross_step = Attend(
        call, query.out, shared.out, fact_rows, fact_columns, (TARGET, SOURCE, False)
    )
    mid = forward_mid(call, job_d.kept, DEC_G + 2, DEC_B + 2)
    job_e = Job(call, (cross_step.mixed, cross_o, [(0, 64)], 0), mid, (None, None, None))

    def onward(get, at):
        place_norms(get, at)
        first_vectors.start(get, at)
        slots.start(get, at)
        pack_1.make(get)
        swap_1.start(get, at)
        count_facts(get)
        fact_copy = push(
            get(fact_own), get(fact_room), get(fact_send).at[0], get(fact_recv).at[0], at["x"]
        )
        fact_copy.start()
        first_vectors.second(get, at)
        swap_1.finish(get, at)
        spread_1.launch(get, at)
        for pack in (pack_o, pack_2):
            pack.make(get)
        first_vectors.finish(get, at)
        slots.finish(get, at)
        job_a.settle(get, at)
        job_c.settle(get, at)
        fact_copy.wait()
        place_facts(get, at)
        job_a.rows_forward(get, at)
        job_c.rows_forward(get, at)
        spread_1.relay(get, at)
        swap_o.start(get, at)
        swap_2.start(get, at)
        for pack in (pack_3, pack_4):
            pack.make(get)
        job_a.collect(get, at)
        job_c.collect(get, at)
        enc_step.prepare(get)
        swap_o.finish(get, at)
        swap_2.finish(get, at)
        job_a.drain()
        job_c.drain()
        spread_1.pass_on(get, at)
        spread_o.launch(get, at)
        spread_2.launch(get, at)
        swap_3.start(get, at)
        swap_4.start(get, at)
        spread_1.finish(get, at)
        for plan in plans:
            plan[1].start(get)
        for rows, weight, queries, keys in plans:
            weight.wait(get)
            for row in range(4):
                for m in range(3):
                    made = nt(get(rows)[row], weight.matrix(get, m * 64, 64))
                    (queries if m == 0 else keys).store(get, at, row, m * 256, made)
        for plan in plans:
            plan[3].finish(get)
        spread_o.relay(get, at)
        enc_step.pairs(get, 0, 2)
        call.save(get, enc_step.mixed)
        spread_o.pass_on(get, at)
        swap_3.finish(get, at)
        swap_4.finish(get, at)
        spread_o.finish(get, at)
        enc_o.start(get)
        self_o.start(get)
        job_b.sums(get, at)
        self_step.prepare(get)
        self_step.pairs(get, 0, 1)
        job_b.sum_forward(get, at)
        self_step.pairs(get, 1, 2)
        call.save(get, self_step.mixed)
        job_b.sum_own(get, at)
        job_d.sums(get, at)
        job_b.settle(get, at)
        spread_2.relay(get, at)
        spread_3.launch(get, at)
        job_d.sum_forward(get, at)
        job_d.sum_own(get, at)
        job_b.rows_forward(get, at)
        job_d.settle(get, at)
        spread_2.pass_on(get, at)
        spread_2.finish(get, at)
        enc_u.start(get)
        enc_d.start(get)
        job_b.collect(get, at)
        job_m.sums(get, at)
        job_d.rows_forward(get, at)
        job_m.sum_forward(get, at)
        job_m.sum_own(get, at)
        spread_3.relay(get, at)
        spread_4.launch(get, at)
        job_m.settle(get, at)
        spread_3.pass_on(get, at)
        spread_3.finish(get, at)
        for weight in (cross_a, cross_b, cross_o):
            weight.start(get)
        job_m.rows_forward(get, at)
        job_d.product(get, at, at["own_row"])
        job_d.collect(get, at)
        job_m.product(get, at, at["own_row"])
        job_m.collect(get, at)
        for job in (job_b, job_d, job_m):
            job.drain()
        shared.finish(get)
        cross_step.prepare(get)
        cross_step.pairs(get, 0, 1)
        spread_4.relay(get, at)
        cross_step.pairs(get, 1, 2)
        call.save(get, cross_step.mixed)
        job_e.sums(get, at)
        job_e.sum_forward(get, at)
        job_e.sum_own(get, at)
        job_e.settle(get, at)
        spread_4.pass_on(get, at)
        job_e.rows_forward(get, at)
        job_e.collect(get, at)
        job_e.drain()
        spread_4.finish(get, at)

    (
        stream_in,
        target_in,
        vectors,
        fact_rows,
        fact_columns,
        unused,
        unused,
        unused,
        unused,
        unused,
        first_w,
        first_o,
        second_w,
        cross_w,
        third_w,
        rows_a,
        rows_c,
        enc_q,
        enc_kv,
        self_q,
        self_kv,
        enc_mixed,
        enc_total,
        self_mixed,
        self_total,
        stream_mid,
        rows_b,
        target_mid,
        cross_q,
        cross_kv,
        rows_d,
        enc_hidden,
        enc_slope,
        stream_end,
        memory,
        cross_mixed,
        cross_total,
        target_late,
        rows_e,
    ) = run_body(call, onward, ["all"], "onward", 0, 170 * MICROSECOND)

    call = Call()
    dec_u, dec_d = pick(call, third_w, UP), pick(call, third_w, DOWN)
    cross_o = pick(call, cross_w, O)
    feed = Feed(call, rows_e, dec_u, dec_d)
    slots = Slots(call, [by_owner(cotangent)], True)
    vec, res, cot = call.take(vectors), call.fetch(target_late), slots.outs[0]
    decoded_out, grad_end = call.keep((128, 1024), BF16), call.hold((128, 1024), F32)
    share_out = call.give((2, 1024), F32)

    def last_mid(get, total):
        stream = get(res)[...] + total
        gain, shift = get(vec)[DEC_G + 3 : DEC_G + 4], get(vec)[DEC_B + 3 : DEC_B + 4]
        unit, unused = unit_of(stream)
        get(decoded_out)[...] = (unit * gain + shift).astype(BF16)
        grad, shares = norm_back(stream, gain, get(cot)[...].astype(F32))
        get(grad_end)[...] = grad
        get(share_out)[...] = shares
        call.save(get, decoded_out)
        return grad.astype(BF16)

    active = deactivated(call, feed.slope)
    job_t = Job(call, feed, last_mid, (dec_d, [(0, 256)], active.store))
    mid = backward_mid(call, target_late, DEC_G + 2, grad_end)
    query = Plain(call, 256)
    job_c = Job(call, (active.out, dec_u, [(0, 256)], 0), mid, (cross_o, [(0, 64)], query.store))
    down_shares = Shares(call, [(feed.hidden, 0, job_t.gathered)], 256, False)
    joined = call.give((4, 4, 512, 128), BF16, pltpu.HBM)
    up_shares = Shares(call, [(active.out, 0, feed.rows)], 256, joined, 0)
    back = AttendBack(
        call,
        cross_q,
        cross_kv,
        query.out,
        cross_total,
        fact_rows,
        fact_columns,
        (TARGET, SOURCE, False),
    )
    cross_shares = Shares(
        call,
        [
            (back.out, 0, rows_d),
            (back.out, 256, memory),
            (back.out, 512, memory),
            (cross_mixed, 0, job_c.gathered),
        ],
        64,
        joined,
        256,
    )
    gather = Gather(call, down_shares.room, 256)

    def turning(get, at):
        for weight in (dec_u, dec_d, cross_o):
            weight.start(get)
        slots.start(get, at)
        job_t.sums(get, at)
        job_t.sum_forward(get, at)
        job_t.sum_own(get, at)
        slots.finish(get, at)
        job_t.settle(get, at)
        job_t.product(get, at, at["own_row"])
        job_t.rows_forward(get, at)
        job_t.collect(get, at)
        job_c.sums(get, at)
        job_c.sum_forward(get, at)
        job_c.sum_own(get, at)
        down_shares.middle(get, at)
        down_shares.finish(get, at)
        job_c.settle(get, at)
        gather.launch(get, at)
        job_c.product(get, at, at["own_row"])
        job_c.rows_forward(get, at)
        up_shares.middle(get, at)
        job_c.collect(get, at)
        up_shares.finish(get, at)
        gather.relay(get, at)
        job_t.drain()
        job_c.drain()
        back.late(get, at)
        cross_shares.middle(get, at)
        cross_shares.finish(get, at)
        gather.finish(get, at)

    (
        dec_hidden,
        dec_slope,
        unused,
        decoded,
        norm_3,
        dec_grad_act,
        grad_rows_e,
        grad_late,
        norm_2,
        cross_grad_mixed,
        grad_rows_d,
        joined_s,
        cross_grads,
        down_g,
    ) = run_body(call, turning, ["all"], "turning", 1, 62 * MICROSECOND)

    call = Call()
    cross_a, cross_b = pick(call, cross_w, Q), pick(call, cross_w, KV)
    self_o, enc_d = pick(call, first_o, FIRST_O, SELF_O), pick(call, second_w, DOWN)
    slots = Slots(call, [decoded], False)
    mid = backward_mid(call, target_mid, DEC_G + 1, grad_late)
    query = Plain(call, 256)
    job_t = Job(call, (cross_grads, cross_a, [(0, 64)], 0), mid, (self_o, [(0, 64)], query.store))
    mid = backward_mid(call, stream_end, ENC_G + 2)
    active = deactivated(call, call.fetch(enc_slope))
    job_s = Job(
        call,
        (cross_grads, cross_b, [(0, 64), (64, 64)], 256),
        mid,
        (enc_d, [(0, 256)], active.store),
    )
    shares = Shares(
        call, [(active.out, 0, rows_b), (enc_hidden, 0, job_s.gathered)], 256
    )
    gather, swap = Gather(call, joined_s, 512), Swap(call, down_g)

    def backing(get, at):
        gather.launch(get, at)
        for weight in (cross_b, cross_a, enc_d, self_o):
            weight.start(get)
        job_s.sums(get, at)
        job_t.sums(get, at)
        job_s.sum_forward(get, at)
        job_t.sum_forward(get, at)
        job_s.sum_own(get, at)
        job_s.settle(get, at)
        job_t.sum_own(get, at)
        job_t.settle(get, at)
        slots.start(get, at)
        job_s.product(get, at, at["own_row"])
        job_s.rows_forward(get, at)
        job_t.product(get, at, at["own_row"])
        job_t.rows_forward(get, at)
        swap.start(get, at)
        job_s.collect(get, at)
        gather.relay(get, at)
        shares.middle(get, at)
        job_t.collect(get, at)
        shares.finish(get, at)
        job_s.drain()
        job_t.drain()
        slots.finish(get, at)
        swap.finish(get, at)
        gather.finish(get, at)

    (
        decoded,
        grad_mid,
        norm_1,
        self_grad_mixed,
        grad_rows_c,
        grad_stream,
        enc_norm_2,
        enc_grad_act,
        grad_rows_b,
        feed_s,
        up_cross_g,
        down_g,
    ) = run_body(call, backing, ["x", "y", "core", "d", "ways"], "backing", 2, 46 * MICROSECOND)

    call = Call()
    enc_u, enc_o = pick(call, second_w, UP), pick(call, first_o, FIRST_O)
    self_a = pick(call, first_w, QKV, SELF)
    self_back = AttendBack(
        call,
        self_q,
        self_kv,
        self_grad_mixed,
        self_total,
        fact_rows,
        fact_columns,
        (TARGET, TARGET, True),
    )
    mid = backward_mid(call, stream_mid, ENC_G + 1, grad_stream)
    query = Plain(call, 256)
    job_s = Job(call, (enc_grad_act, enc_u, [(0, 256)], 0), mid, (enc_o, [(0, 64)], query.store))
    mid = backward_mid(call, target_in, DEC_G, grad_mid, BF16)
    job_t = Job(call, (self_back.out, self_a, [(0, 64), (64, 64), (128, 64)], 0), mid, None)
    self_shares = Shares(
        call,
        [
            (self_back.out, 0, rows_c),
            (self_back.out, 256, rows_c),
            (self_back.out, 512, rows_c),
            (self_mixed, 0, grad_rows_c),
        ],
        64,
        False,
    )
    enc_back = AttendBack(
        call,
        enc_q,
        enc_kv,
        query.out,
        enc_total,
        fact_rows,
        fact_columns,
        (SOURCE, SOURCE, False),
    )
    enc_shares = Shares(
        call,
        [
            (enc_back.out, 0, rows_a),
            (enc_back.out, 256, rows_a),
            (enc_back.out, 512, rows_a),
            (enc_mixed, 0, job_s.gathered),
        ],
        64,
        False,
    )
    enc_a = pick(call, first_w, QKV)
    mid = backward_mid(call, stream_in, ENC_G, job_s.kept, BF16)
    job_f = Job(call, (enc_back.out, enc_a, [(0, 64), (64, 64), (128, 64)], 0), mid, None)
    gather_f, gather_s = Gather(call, feed_s, 512), Gather(call, self_shares.room, 256)
    gather_e = Gather(call, enc_shares.room, 256)
    for gather, rows in ((gather_f, 512), (gather_s, 256), (gather_e, 256)):
        call.rows_of[gather.out] = rows
    swap, swap_f = Swap(call, up_cross_g), Swap(call, gather_f.out)
    swap_s, swap_e = Swap(call, gather_s.out), Swap(call, gather_e.out)
    target_slots, source_slots = Slots(call, [job_t.kept], False), Slots(call, [job_f.kept], False)
    others = [call.take(norm) for norm in (norm_1, norm_2, norm_3, enc_norm_2)]
    norm_sum = call.hold((16, 1024), F32)
    sums = Vectors(call, norm_sum, False)

    def selfward(get, at):
        gather_f.launch(get, at)
        for weight in (enc_u, self_a, enc_o, enc_a):
            weight.start(get)
        self_back.prepare(get)
        job_s.sums(get, at)
        self_back.pair(get, at, 0)
        job_s.sum_forward(get, at)
        self_back.pair(get, at, 1)
        self_back.end(get)
        job_s.sum_own(get, at)
        job_t.sums(get, at)
        job_s.settle(get, at)
        job_t.sum_forward(get, at)
        job_t.sum_own(get, at)
        self_shares.middle(get, at)
        self_shares.finish(get, at)
        gather_s.launch(get, at)
        job_s.product(get, at, at["own_row"])
        job_s.rows_forward(get, at)
        job_t.settle(get, at)
        gather_f.relay(get, at)
        target_slots.start(get, at)
        swap.start(get, at)
        job_s.collect(get, at)
        job_s.drain()
        job_t.drain()
        enc_back.late(get, at)
        enc_shares.middle(get, at)
        enc_shares.finish(get, at)
        gather_e.launch(get, at)
        gather_s.relay(get, at)
        job_f.sums(get, at)
        job_f.sum_forward(get, at)
        job_f.sum_own(get, at)
        job_f.settle(get, at)
        gather_e.relay(get, at)
        source_slots.start(get, at)
        total = get(norm_sum)
        for row, shares in (
            (0, get(job_f.shares)),
            (1, get(job_s.shares)),
            (2, get(others[3])),
            (6, get(job_t.shares)),
            (7, get(others[0])),
            (8, get(others[1])),
            (9, get(others[2])),
        ):
            below = row + (3 if row < 6 else 4)
            total[row : row + 1] = shares[0:1]
            total[below : below + 1] = shares[1:2]
        total[14:16] = jnp.zeros((2, 1024), F32)
        sums.start(get, at)
        job_f.drain()
        gather_f.finish(get, at)
        swap_f.start(get, at)
        sums.second(get, at)
        target_slots.finish(get, at)
        gather_s.finish(get, at)
        swap_s.start(get, at)
        sums.finish(get, at)
        source_slots.finish(get, at)
        swap.finish(get, at)
        swap_f.finish(get, at)
        gather_e.finish(get, at)
        swap_e.start(get, at)
        swap_s.finish(get, at)
        swap_e.finish(get, at)

    made = run_body(call, selfward, ["all"], "selfward", 3, 105 * MICROSECOND)
    up_cross_g, feed_g, self_g, enc_g, target_grad, source_grad, norm_grad = made[-7:]
    norm_grad = norm_grad.reshape(16, copies, 4, 32 // copies)
    if copies > 1:
        norm_grad = lax.psum_scatter(norm_grad, "k", scatter_dimension=1)
    norm_grad = norm_grad.reshape(16, 4, -1)
    norm_grad = lax.dynamic_index_in_dim(norm_grad, z, 1, False)

    (
        dec_d,
        dec_u,
        cross_a,
        cross_o,
        enc_u,
        enc_d,
        self_a,
        self_o,
        enc_a,
        enc_o,
        source_grad,
        target_grad,
    ) = unpacked(
        [down_g, up_cross_g, feed_g, self_g, enc_g],
        [source_grad, target_grad],
        [("down",), ("up", "q", "o"), ("up", "down"), ("q", "o"), ("q", "o")],
    )

    def narrow(array, axis):
        if copies == 1:
            return array
        return lax.psum_scatter(array, "k", scatter_dimension=axis, tiled=True)

    enc_a, self_a, cross_a = (narrow(array, 1) for array in (enc_a, self_a, cross_a))
    enc_o, self_o, cross_o = (narrow(array, 1) for array in (enc_o, self_o, cross_o))
    enc_u, dec_u = narrow(enc_u, 0), narrow(dec_u, 0)
    enc_d, dec_d = narrow(enc_d, 1), narrow(dec_d, 1)
    return (
        by_owner(decoded, True),
        by_owner(source_grad, True),
        by_owner(target_grad, True),
        enc_a,
        enc_o,
        enc_u,
        enc_d,
        norm_grad[:3],
        norm_grad[3:6],
        self_a,
        self_o,
        cross_a,
        cross_o,
        dec_u,
        dec_d,
        norm_grad[6:10],
        norm_grad[10:14],
    )


def solution(mesh):
    dp, seq, mp = (mesh.shape[name] for name in ("dp", "seq", "mp"))
    assert dp % 2 == 0 and seq == 4 and mp == 4
    fine = Mesh(mesh.devices.reshape(2, dp // 2, 2, 2, 4), AXES)
    d, s = ("hi", "k"), ("y", "c")
    rows = P(d, s + ("mp",), None)
    three, flat = P(None, d + s, "mp"), P("mp", d + s)
    up, vector = P(d + s, "mp"), P(None, d + s + ("mp",))
    attention, feeding = (three, flat), (up, flat)
    return jax.shard_map(
        local,
        mesh=fine,
        in_specs=(rows,) * 3
        + (P(d), P(d), P(d, None), P(d, None))
        + attention
        + feeding
        + (vector, vector)
        + attention * 2
        + feeding
        + (vector, vector),
        out_specs=(rows,) * 3
        + attention
        + feeding
        + (vector, vector)
        + attention * 2
        + feeding
        + (vector, vector),
        check_vma=False,
    )
```

profile of v0, /device:TPU:0, one launch (start us, length us, event | category | flops | bytes accessed | tf_op | source)
XLA Modules:
  0.0 403.3 jit_solution(15784291546231467229)
XLA Ops:
  0.7 177.8 %onward.1 = (bf16[128,1024]{1,0:T(8,128)(2,1)}, bf16[128,1024]{1,0:T(8,128)(2,1)}, f32[16,1024]{1,0:T(8,128)}, f32[8,1024]{1,0:T(8,128)}, f32[1024,128]{1,0:T(8,...) custom-call(bf16[2,64,1024]{2,1,0:T(8,128)(2,1)} %refs_0_.1, ...), custom_call_target="tpu_custom_call" | custom-call | flops 170000007168 | tf_op jit(solution)/shard_map/onward/pallas_call | solution.py:110
  178.5 0.0 copy-start
  178.5 0.8 copy-done
  179.3 0.0 copy-start.1
  179.3 0.8 copy-done.1
  180.1 0.0 copy-start.2
  180.1 0.7 copy-done.2
  180.8 65.2 %turning.1 = (bf16[4,128,1024]{2,1,0:T(8,128)(2,1)}, f32[4,128,1024]{2,1,0:T(8,128)}, bf16[128,1024]{1,0:T(8,128)(2,1)}, bf16[128,1024]{1,0:T(8,128)(2,1)}, f32[...) custom-call(bf16[2,4,4,512,128]{4,3,2,1,0:T(8,128)(2,1)} %get-tuple-, ...), custom_call_target="tpu_custom_call" | custom-call | flops 62000001024 | tf_op jit(solution)/shard_map/turning/pallas_call | solution.py:110
  246.0 0.0 copy-start.5
  246.0 0.0 copy-start.6
  246.0 55.1 %backing.1 = (bf16[2,64,1024]{2,1,0:T(8,128)(2,1)}, f32[128,1024]{1,0:T(8,128)}, f32[2,1024]{1,0:T(2,128)S(1)}, bf16[4,128,256]{2,1,0:T(8,128)(2,1)}, bf16[4,128...) custom-call(bf16[2,4,4,256,128]{4,3,2,1,0:T(8,128)(2,1)} %get-tuple-, ...), custom_call_target="tpu_custom_call" | custom-call | flops 46000001024 | tf_op jit(solution)/shard_map/backing/pallas_call | solution.py:110
  301.1 0.0 copy-done.5
  301.1 0.0 copy-done.6
  301.1 0.0 copy-start.3
  301.1 0.6 copy-done.3
  301.7 0.0 copy-start.4
  301.7 0.6 copy-done.4
  302.3 93.6 %selfward.1 = (bf16[4,128,768]{2,1,0:T(8,128)(2,1)}, f32[128,1024]{1,0:T(8,128)}, f32[2,1024]{1,0:T(2,128)}, bf16[4,128,256]{2,1,0:T(8,128)(2,1)}, bf16[4,128,10...) custom-call(bf16[2,4,4,512,128]{4,3,2,1,0:T(8,128)(2,1)} %get-tuple-, ...), custom_call_target="tpu_custom_call" | custom-call | flops 105000001536 | tf_op jit(solution)/shard_map/selfward/pallas_call | solution.py:110
  395.9 0.8 reshape_reshape.3
  396.7 0.6 copy_bitcast_fusion
  397.3 0.0 copy-start.7
  397.3 4.3 %unpacked.1 = (f32[1024,128]{1,0:T(8,128)}, f32[128,1024]{1,0:T(8,128)}, f32[3,128,256]{2,1,0:T(8,128)}, f32[256,128]{1,0:T(8,128)}, f32[128,1024]{1,0:T(8,128)}...) custom-call(bf16[2,64,1024]{2,1,0:T(8,128)(2,1)} %get-tuple-element., ...), custom_call_target="tpu_custom_call" | custom-call | flops 4000000000 | tf_op jit(solution)/shard_map/unpacked/pallas_call | solution.py:110
  401.6 0.6 constant_dynamic-slice_fusion.3
  402.2 0.0 copy-done.7
  402.2 0.7 copy.47
  (1 shorter events, 0.0 us)
Async XLA Ops:
  178.5 0.8 copy-start
  179.3 0.8 copy-start.1
  180.1 0.7 copy-start.2
  246.0 55.1 %copy-start.5 = (f32[2,1024]{1,0:T(2,128)}, f32[2,1024]{1,0:T(2,128)S(1)}, u32[]{:S(2)}) copy-start(f32[2,1024]{1,0:T(2,128)S(1)} %get-tuple-element.137.refs_28_) | copy-start | bytes 24580
  246.0 55.1 %copy-start.6 = (f32[2,1024]{1,0:T(2,128)}, f32[2,1024]{1,0:T(2,128)S(1)}, u32[]{:S(2)}) copy-start(f32[2,1024]{1,0:T(2,128)S(1)} %get-tuple-element.136.refs_27_) | copy-start | bytes 24580
  301.1 0.6 copy-start.3
  301.7 0.6 copy-start.4
  397.3 4.9 %copy-start.7 = (bf16[2,64,1024]{2,1,0:T(8,128)(2,1)S(1)}, bf16[2,64,1024]{2,1,0:T(8,128)(2,1)}, u32[]{:S(2)}) copy-start(bf16[2,64,1024]{2,1,0:T(8,128)(2,1)} %get-tuple-element.182) | copy-start | bytes 786436
where the time goes:
time: 411 us; the launch traced here: 403 us
  Pallas kernels  396 us (96%)
  local copies, waits for them, and re-layouts  6.19 us (2%)
    pallas_call x5, Pallas kernels, run(): pl.pallas_call(kernel, out_shape=tuple(self.shapes), in_specs=self.specs,...  396 us

commit v1 on v0

--- a/solution.py
+++ b/solution.py
@@ -491,21 +491,26 @@
     def __init__(self, call, queries, key_value, rows, columns, kinds):
         self.call, self.kinds = call, kinds
         self.queries, self.key_value = call.fetch(queries), call.fetch(key_value)
-        self.rows, self.columns = call.take(rows), call.fetch(columns)
+        self.rows, self.columns = call.fetch(rows), call.fetch(columns)
         self.mixed = call.keep((4, 128, 256), BF16)
-        self.total = call.give((8, 512), F32)
+        self.total = call.keep((8, 512), F32)
         self.bias = call.hold((1024, 512), F32)
 
     def late(self, get, at):
         self.prepare(get)
         self.pairs(get, 0, 2)
+        self.save(get)
+
+    def save(self, get):
         self.call.save(get, self.mixed)
+        self.call.save(get, self.total)
 
     def visible(self, block):
         return 2 if self.kinds[2] and block == 0 else 4
 
     def prepare(self, get):
-        mask = get(self.bias)
+        mask, total = get(self.bias), get(self.total)
+        total[4:8] = jnp.zeros((4, 512), F32)
         mask[...] = allowed_bias(get(self.rows), get(self.columns), *self.kinds)
 
     def pairs(self, get, first, last):
@@ -543,8 +548,8 @@
     def __init__(self, call, queries, key_value, grad_mixed, total, rows, columns, kinds):
         self.call, self.kinds = call, kinds
         self.queries, self.key_value = call.fetch(queries), call.fetch(key_value)
-        self.grad_mixed, self.total = call.fetch(grad_mixed), call.take(total)
-        self.rows, self.columns = call.take(rows), call.fetch(columns)
+        self.grad_mixed, self.total = call.fetch(grad_mixed), call.fetch(total)
+        self.rows, self.columns = call.fetch(rows), call.fetch(columns)
         self.out = call.keep((4, 128, 768), BF16)
         self.bias, self.sums = call.hold((1024, 512), F32), call.hold((1024, 512), F32)
         self.away, self.landed = call.hold((2, 512, 256), BF16), call.hold((2, 512, 256), BF16)
@@ -997,7 +1002,7 @@
     def __init__(self, call, vectors, inward):
         self.inward = inward
         self.source = call.take(vectors)
-        self.out = call.give((16, 1024) if inward else (16, 128), F32)
+        self.out = call.keep((16, 1024), F32) if inward else call.give((16, 128), F32)
         self.landed, self.whole = call.hold((7, 16, 128), F32), call.hold((16, 128), F32)
         self.split, self.along = call.hold((8, 16, 128), F32), call.hold((3, 16, 128), F32)
         self.send_sem, self.recv_sem = call.sems(10), call.sems(10)
@@ -1174,7 +1179,7 @@
         return Weight(call, packed, base + span[0], span[1])
 
     def forward_mid(call, residual, gain, shift, normed=None):
-        vec, res = call.take(vectors), call.fetch(residual)
+        vec, res = call.fetch(vectors), call.fetch(residual)
         kept = call.keep((128, 1024), F32)
 
         def mid(get, total):
@@ -1192,9 +1197,9 @@
         return mid
 
     def backward_mid(call, stream, gain, residual=None, dtype=F32):
-        vec, kept = call.take(vectors), call.fetch(stream)
+        vec, kept = call.fetch(vectors), call.fetch(stream)
         res = None if residual is None else call.fetch(residual)
-        grad_out, share_out = call.keep((128, 1024), dtype), call.give((2, 1024), F32)
+        grad_out, share_out = call.keep((128, 1024), dtype), call.keep((2, 1024), F32)
 
         def mid(get, total):
             grad, shares = norm_back(get(kept)[...].astype(F32), get(vec)[gain : gain + 1], total)
@@ -1203,6 +1208,7 @@
             get(grad_out)[...] = grad.astype(dtype)
             call.save(get, grad_out)
             get(share_out)[...] = shares
+            call.save(get, share_out)
             return grad.astype(BF16)
 
         mid.kept, mid.shares = grad_out, share_out
@@ -1225,7 +1231,7 @@
     fact_ids = [call.take(source_seg), call.take(target_seg)]
     fact_lengths = [call.take(source_len, pltpu.SMEM), call.take(target_len, pltpu.SMEM)]
     fact_own, fact_room = call.hold((2, 8, 128), F32), call.hold((2, 8, 128), F32)
-    fact_rows, fact_columns = call.give((8, 1024), F32), call.keep((1024, 128), F32)
+    fact_rows, fact_columns = call.keep((8, 1024), F32), call.keep((1024, 128), F32)
     fact_send, fact_recv = call.sems(1), call.sems(1)
 
     def three(array):
@@ -1301,6 +1307,7 @@
             wide = jnp.where(lane == i, down[i], wide)
         columns[...] = wide
         call.save(get, fact_columns)
+        call.save(get, fact_rows)
 
     def first_mid(stream, gain, shift):
         def mid(get, total):
@@ -1359,6 +1366,7 @@
         for pack in (pack_o, pack_2):
             pack.make(get)
         first_vectors.finish(get, at)
+        call.save(get, first_vectors.out)
         slots.finish(get, at)
         job_a.settle(get, at)
         job_c.settle(get, at)
@@ -1396,7 +1404,7 @@
             plan[3].finish(get)
         spread_o.relay(get, at)
         enc_step.pairs(get, 0, 2)
-        call.save(get, enc_step.mixed)
+        enc_step.save(get)
         spread_o.pass_on(get, at)
         swap_3.finish(get, at)
         swap_4.finish(get, at)
@@ -1408,7 +1416,7 @@
         self_step.pairs(get, 0, 1)
         job_b.sum_forward(get, at)
         self_step.pairs(get, 1, 2)
-        call.save(get, self_step.mixed)
+        self_step.save(get)
         job_b.sum_own(get, at)
         job_d.sums(get, at)
         job_b.settle(get, at)
@@ -1446,7 +1454,7 @@
         cross_step.pairs(get, 0, 1)
         spread_4.relay(get, at)
         cross_step.pairs(get, 1, 2)
-        call.save(get, cross_step.mixed)
+        cross_step.save(get)
         job_e.sums(get, at)
         job_e.sum_forward(get, at)
         job_e.sum_own(get, at)
@@ -1504,9 +1512,9 @@
     cross_o = pick(call, cross_w, O)
     feed = Feed(call, rows_e, dec_u, dec_d)
     slots = Slots(call, [by_owner(cotangent)], True)
-    vec, res, cot = call.take(vectors), call.fetch(target_late), slots.outs[0]
+    vec, res, cot = call.fetch(vectors), call.fetch(target_late), slots.outs[0]
     decoded_out, grad_end = call.keep((128, 1024), BF16), call.hold((128, 1024), F32)
-    share_out = call.give((2, 1024), F32)
+    share_out = call.keep((2, 1024), F32)
 
     def last_mid(get, total):
         stream = get(res)[...] + total
@@ -1517,6 +1525,7 @@
         get(grad_end)[...] = grad
         get(share_out)[...] = shares
         call.save(get, decoded_out)
+        call.save(get, share_out)
         return grad.astype(BF16)
 
     active = deactivated(call, feed.slope)
@@ -1724,7 +1733,7 @@
     swap, swap_f = Swap(call, up_cross_g), Swap(call, gather_f.out)
     swap_s, swap_e = Swap(call, gather_s.out), Swap(call, gather_e.out)
     target_slots, source_slots = Slots(call, [job_t.kept], False), Slots(call, [job_f.kept], False)
-    others = [call.take(norm) for norm in (norm_1, norm_2, norm_3, enc_norm_2)]
+    others = [call.fetch(norm) for norm in (norm_1, norm_2, norm_3, enc_norm_2)]
     norm_sum = call.hold((16, 1024), F32)
     sums = Vectors(call, norm_sum, False)
 

time: 411 us -> 407 us (level)
  no operation moved by 1% of the time
where the time goes in v1:
time: 407 us; the launch traced here: 399 us
  Pallas kernels  395 us (97%)
    pallas_call x5, Pallas kernels, run(): pl.pallas_call(kernel, out_shape=tuple(self.shapes), in_specs=self.specs,...  395 us

profile of v1, /device:TPU:0, one launch (start us, length us, event | category | flops | bytes accessed | tf_op | source)
XLA Modules:
  0.0 399.2 jit_solution(13593372354992984915)
XLA Ops:
  0.7 177.2 %onward.1 = (bf16[128,1024]{1,0:T(8,128)(2,1)}, bf16[128,1024]{1,0:T(8,128)(2,1)}, f32[16,1024]{1,0:T(8,128)}, f32[8,1024]{1,0:T(8,128)}, f32[1024,128]{1,0:T(8,...) custom-call(bf16[2,64,1024]{2,1,0:T(8,128)(2,1)} %refs_0_.1, ...), custom_call_target="tpu_custom_call" | custom-call | flops 170000007168 | tf_op jit(solution)/shard_map/onward/pallas_call | solution.py:110
  177.9 65.5 %turning.1 = (bf16[4,128,1024]{2,1,0:T(8,128)(2,1)}, f32[4,128,1024]{2,1,0:T(8,128)}, bf16[128,1024]{1,0:T(8,128)(2,1)}, bf16[128,1024]{1,0:T(8,128)(2,1)}, f32[...) custom-call(bf16[2,4,4,512,128]{4,3,2,1,0:T(8,128)(2,1)} %get-tuple-, ...), custom_call_target="tpu_custom_call" | custom-call | flops 62000001024 | tf_op jit(solution)/shard_map/turning/pallas_call | solution.py:110
  243.4 55.4 %backing.1 = (bf16[2,64,1024]{2,1,0:T(8,128)(2,1)}, f32[128,1024]{1,0:T(8,128)}, f32[2,1024]{1,0:T(2,128)}, bf16[4,128,256]{2,1,0:T(8,128)(2,1)}, bf16[4,128,102...) custom-call(bf16[2,4,4,256,128]{4,3,2,1,0:T(8,128)(2,1)} %get-tuple-, ...), custom_call_target="tpu_custom_call" | custom-call | flops 46000001024 | tf_op jit(solution)/shard_map/backing/pallas_call | solution.py:110
  298.8 93.0 %selfward.1 = (bf16[4,128,768]{2,1,0:T(8,128)(2,1)}, f32[128,1024]{1,0:T(8,128)}, f32[2,1024]{1,0:T(2,128)}, bf16[4,128,256]{2,1,0:T(8,128)(2,1)}, bf16[4,128,10...) custom-call(bf16[2,4,4,512,128]{4,3,2,1,0:T(8,128)(2,1)} %get-tuple-, ...), custom_call_target="tpu_custom_call" | custom-call | flops 105000001536 | tf_op jit(solution)/shard_map/selfward/pallas_call | solution.py:110
  391.8 0.8 reshape_reshape.3
  392.6 0.6 copy_bitcast_fusion
  393.2 0.0 copy-start
  393.2 4.3 %unpacked.1 = (f32[1024,128]{1,0:T(8,128)}, f32[128,1024]{1,0:T(8,128)}, f32[3,128,256]{2,1,0:T(8,128)}, f32[256,128]{1,0:T(8,128)}, f32[128,1024]{1,0:T(8,128)}...) custom-call(bf16[2,64,1024]{2,1,0:T(8,128)(2,1)} %get-tuple-element., ...), custom_call_target="tpu_custom_call" | custom-call | flops 4000000000 | tf_op jit(solution)/shard_map/unpacked/pallas_call | solution.py:110
  397.5 0.6 constant_dynamic-slice_fusion.3
  398.1 0.0 copy-done
  398.1 0.7 copy.47
  (1 shorter events, 0.0 us)
Async XLA Ops:
  393.2 4.9 %copy-start = (bf16[2,64,1024]{2,1,0:T(8,128)(2,1)S(1)}, bf16[2,64,1024]{2,1,0:T(8,128)(2,1)}, u32[]{:S(2)}) copy-start(bf16[2,64,1024]{2,1,0:T(8,128)(2,1)} %get-tuple-element.182) | copy-start | bytes 786436
